TPU v7x, 512 devices: a whole 4x4x16 slice. The times are simulated.
512 devices in a mesh: tile: 64 (over x, z_lo, core), tm: 8 (over z_hi, y).
Axes of the slice: x: 4, y: 4, z: 16 (z_hi: 2, z_lo: 8; z = z_hi * 8 + z_lo), core: 2. Of those that a mesh axis runs over, the one named last changes fastest.
Arguments:
- controls: float32 [16, 512, 8, 512], P('tm', 'tile'), may hold values from -6 to 6
- perturbations: bfloat16 [8, 16, 4, 512, 8, 512], P('tm', None, None, 'tile'), may hold values from -6 to 6
- owner: int32 [16], replicated, may hold values from 0 to 15, each once
- land_mask: int32 [512, 512], P('tile'), may hold values 0 or 1
- diffusivity: float32 [2, 8], replicated, may hold values from 0.2 to 0.24
Outputs:
- increment: float32 [8, 4, 512, 8, 512], P('tm', None, 'tile')
Inputs may be any that keep to these rules, and one draw needn't show every extreme that they name: owner names every member exactly once.
All inputs are finite; a program needn't handle non-finite values. No bound on the sum of `land_mask` on one device may be relied on, other than what follows from the above.
Results may differ from a plain program's by a relative error of at most 0.0029.
Values may be sent and summed in bfloat16 or wider, within the bound.
A program may use at most 64 MiB of HBM per device.

v0:
```python
import math
import jax
import jax.numpy as jnp
from jax import lax
from jax.sharding import PartitionSpec as P

SWEEPS = 4


def with_halo(cells, sides, width):
    for axis, dim in sides:
        count = lax.axis_size(axis)
        ends = count - 1
        head = lax.slice_in_dim(cells, 0, width, axis=dim)
        tail = lax.slice_in_dim(cells, cells.shape[dim] - width, cells.shape[dim], axis=dim)
        cells = jnp.concatenate(
            [
                lax.ppermute(tail, axis, [(i, (i + 1) % count) for i in range(ends)]),
                cells,
                lax.ppermute(head, axis, [((i + 1) % count, i) for i in range(ends)]),
            ],
            axis=dim,
        )
    return cells


def spread(value, axis, source):
    kept = jnp.where(lax.axis_index(axis) == source, value, 0).astype(value.dtype)
    return lax.psum(kept, axis)


def weight_sweep(field, coef):
    padded = jnp.pad(field, ((0, 0), (1, 1), (0, 0), (1, 1)))
    coef_pad = jnp.pad(coef, ((1, 1), (0, 0), (1, 1)))
    flux = 0.5 * (coef + coef_pad[:-2, :, 1:-1]) * (padded[:, :-2, :, 1:-1] - field)
    flux = flux + 0.5 * (coef + coef_pad[2:, :, 1:-1]) * (padded[:, 2:, :, 1:-1] - field)
    flux = flux + 0.5 * (coef + coef_pad[1:-1, :, :-2]) * (padded[:, 1:-1, :, :-2] - field)
    flux = flux + 0.5 * (coef + coef_pad[1:-1, :, 2:]) * (padded[:, 1:-1, :, 2:] - field)
    return field + flux


def on_device(controls, perturbations, owner, land_mask, diffusivity):
    diffuse_coef = jnp.where(
        land_mask[:, None, :] == 1, diffusivity[1][None, :, None], diffusivity[0][None, :, None]
    )
    rim_rows = 1
    coef_wide = with_halo(diffuse_coef, (("tile", 0),), rim_rows)
    smooth = controls
    for sweep_index in range(SWEEPS):
        extended = with_halo(smooth, (("tile", 1),), 1)
        smooth = weight_sweep(extended, coef_wide)[:, 1:-1]
    weights = smooth.astype(jnp.bfloat16)
    member_count = owner.shape[0]
    pert_here = perturbations[0]
    factor = 1.0 / math.sqrt(member_count - 1)
    pair_count = controls.shape[0]
    summed = jnp.zeros(pert_here.shape[1:], jnp.float32)
    for root_index in range(lax.axis_size("tm")):
        arrived = spread(weights, "tm", root_index)
        chosen = lax.dynamic_slice_in_dim(owner, root_index * pair_count, pair_count)
        selected = jnp.take(pert_here, chosen, axis=0)
        summed = summed + jnp.einsum(
            "pvxly,pxly->vxly", selected, arrived, preferred_element_type=jnp.float32
        )
    return (summed * factor)[None]


def solution(mesh):
    return jax.shard_map(
        on_device,
        mesh=mesh,
        in_specs=(
            P("tm", "tile", None, None),
            P("tm", None, None, "tile", None, None),
            P(),
            P("tile", None),
            P(),
        ),
        out_specs=P("tm", None, "tile", None, None),
        check_vma=False,
    )
```

profile of v0, /device:TPU:24, one launch (start us, length us, event | category | flops | bytes accessed | tf_op | source)
XLA Modules:
  0.0 285.7 jit_solution(9800533867567195115)
XLA Ops:
  6.5 0.8 slice_bitcast_fusion.1
  7.3 0.7 broadcast_compare_fusion
  8.1 1.7 collective-permute-start.2
  9.9 1.3 collective-permute-start.3
  11.2 0.8 fusion.57
  11.9 4.7 %collective-permute-start = (f32[2,1,8,512]{3,2,1,0:T(8,128)S(1)}, f32[2,1,8,512]{3,2,1,0:T(8,128)S(1)}, u32[]{:S(2)}, u32[]{:S(2)}) collective-permute-start(f32[2,1,8,512]{3,2,1,0:T(8,128)S(1)} %get-tuple-element.43), channel_id=1, source_target_pairs={{0,8},{8,16},{16,24},{24,32},{32,40},{40,48},{48,56},{56,64},{64,7... | collective-permute-start | bytes 98312 | tf_op jit(solution)/shard_map/ppermute | solution.py:18
  16.7 1.3 collective-permute-start.1
  18.0 0.2 fusion.46
  18.2 1.0 constant_dynamic-update-slice_fusion.1
  19.2 1.8 collective-permute-done.1
  21.0 0.3 fusion.5
  21.3 4.5 %collective-permute-start.4 = (f32[2,1,8,512]{3,2,1,0:T(8,128)S(1)}, f32[2,1,8,512]{3,2,1,0:T(8,128)S(1)}, u32[]{:S(2)}, u32[]{:S(2)}) collective-permute-start(f32[2,1,8,512]{3,2,1,0:T(8,128)S(1)} %get-tuple-element.40), channel_id=1, source_target_pairs={{0,8},{8,16},{16,24},{24,32},{32,40},{40,48},{48,56},{56,64},{64,7... | collective-permute-start | bytes 98312 | tf_op jit(solution)/shard_map/ppermute | solution.py:18
  25.8 1.3 collective-permute-start.5
  27.2 1.8 collective-permute-done.5
  29.0 0.3 fusion.17
  29.3 4.3 %collective-permute-start.6 = (f32[2,1,8,512]{3,2,1,0:T(8,128)S(1)}, f32[2,1,8,512]{3,2,1,0:T(8,128)S(1)}, u32[]{:S(2)}, u32[]{:S(2)}) collective-permute-start(f32[2,1,8,512]{3,2,1,0:T(8,128)S(1)} %get-tuple-element.38), channel_id=1, source_target_pairs={{0,8},{8,16},{16,24},{24,32},{32,40},{40,48},{48,56},{56,64},{64,7... | collective-permute-start | bytes 98312 | tf_op jit(solution)/shard_map/ppermute | solution.py:18
  33.6 1.3 collective-permute-start.7
  34.9 1.8 collective-permute-done.7
  36.7 0.3 fusion.29
  37.0 4.3 %collective-permute-start.8 = (f32[2,1,8,512]{3,2,1,0:T(8,128)S(1)}, f32[2,1,8,512]{3,2,1,0:T(8,128)S(1)}, u32[]{:S(2)}, u32[]{:S(2)}) collective-permute-start(f32[2,1,8,512]{3,2,1,0:T(8,128)S(1)} %get-tuple-element.36), channel_id=1, source_target_pairs={{0,8},{8,16},{16,24},{24,32},{32,40},{40,48},{48,56},{56,64},{64,7... | collective-permute-start | bytes 98312 | tf_op jit(solution)/shard_map/ppermute | solution.py:18
  41.4 1.3 collective-permute-start.9
  42.8 1.7 collective-permute-done.9
  44.5 0.3 fusion.36
  44.8 0.9 broadcast_select_fusion.6
  45.6 1.0 broadcast_select_fusion.7
  46.6 0.1 compare_and_fusion.6
  46.7 2.8 gather_fusion.1
  49.5 2.8 gather_fusion
  52.3 2.8 gather_fusion.2
  55.1 2.8 gather_fusion.3
  57.9 3.6 %gather_fusion.4 = bf16[2,4,8,8,512]{4,3,2,1,0:T(8,128)(2,1)} fusion(bf16[16,4,8,8,512]{4,3,2,1,0:T(8,128)(2,1)} %bitcast.45, s32[1024]{0:T(1024)S(1)} %get-tuple-element.84), kind=kCustom, calls=%fused_computation.4.clone | custom fusion | bytes 1048584 | tf_op jit(solution)/shard_map/jit(_take)/gather | solution.py:61
  61.4 2.8 gather_fusion.5
  64.2 3.6 %gather_fusion.6 = bf16[2,4,8,8,512]{4,3,2,1,0:T(8,128)(2,1)} fusion(bf16[16,4,8,8,512]{4,3,2,1,0:T(8,128)(2,1)} %bitcast.47, s32[1024]{0:T(1024)S(1)} %get-tuple-element.82), kind=kCustom, calls=%fused_computation.6.clone | custom fusion | bytes 1048584 | tf_op jit(solution)/shard_map/jit(_take)/gather | solution.py:61
  67.8 2.8 gather_fusion.7
  70.6 200.8 %all-reduce.8.cloned.1.call-done = (bf16[2,8,8,512]{3,2,1,0:T(8,128)(2,1)}, bf16[2,8,8,512]{3,2,1,0:T(8,128)(2,1)}, bf16[2,8,8,512]{3,2,1,0:T(8,128)(2,1)}, bf16...) async-done(((bf16[2,8,8,512]{3,2,1,0:T(8,128)(2,1)}, ...) | async-done | bytes 1048592 | tf_op jit(solution)/shard_map/psum | solution.py:29
  271.3 1.1 bitcast_convert_fusion.6
  272.4 1.0 bitcast_convert_fusion.4
  273.4 1.0 bitcast_convert_fusion.2
  274.5 1.1 bitcast_convert_fusion
  275.6 0.2 multiply_reduce_fusion.6
  275.8 0.2 multiply_reduce_fusion.7
  276.1 0.2 multiply_reduce_fusion.5
  276.3 0.2 multiply_reduce_fusion.4
  276.6 0.2 multiply_reduce_fusion.3
  276.8 0.2 multiply_reduce_fusion.2
  277.1 0.2 multiply_reduce_fusion.1
  277.3 0.2 multiply_reduce_fusion
  277.5 1.3 multiply_bitcast_fusion
  (36 shorter events, 0.4 us)
Async XLA Ops:
  6.5 264.8 %all-reduce.8.cloned.1.call-start = ((), (), s32[]{:S(2)}) async-start(), calls=%async_computation | async-start | bytes 2097152 | tf_op jit(solution)/shard_map/psum | solution.py:29
  8.1 9.9 %collective-permute-start.2 = (f32[1,8,512]{2,1,0:T(8,128)S(1)}, f32[1,8,512]{2,1,0:T(8,128)S(1)}, u32[]{:S(2)}, u32[]{:S(2)}) collective-permute-start(f32[1,8,512]{2,1,0:T(8,128)S(1)} %get-tuple-element.55), channel_id=1, source_target_pairs={{0,8},{8,16},{16,24},{24,32},{32,40},{40,48},{48,56},{56,64},{64,7... | collective-permute-start | bytes 49160 | tf_op jit(solution)/shard_map/ppermute | solution.py:18
  9.9 8.1 %collective-permute-start.3 = (f32[1,8,512]{2,1,0:T(8,128)S(1)}, f32[1,8,512]{2,1,0:T(8,128)S(1)}, u32[]{:S(2)}, u32[]{:S(2)}) collective-permute-start(f32[1,8,512]{2,1,0:T(8,128)S(1)} %get-tuple-element.56), channel_id=1, source_target_pairs={{8,0},{16,8},{24,16},{32,24},{40,32},{48,40},{56,48},{64,56},{72,6... | collective-permute-start | bytes 49160 | tf_op jit(solution)/shard_map/ppermute | solution.py:20
  11.9 6.2 %collective-permute-start = (f32[2,1,8,512]{3,2,1,0:T(8,128)S(1)}, f32[2,1,8,512]{3,2,1,0:T(8,128)S(1)}, u32[]{:S(2)}, u32[]{:S(2)}) collective-permute-start(f32[2,1,8,512]{3,2,1,0:T(8,128)S(1)} %get-tuple-element.43), channel_id=1, source_target_pairs={{0,8},{8,16},{16,24},{24,32},{32,40},{40,48},{48,56},{56,64},{64,7... | collective-permute-start | bytes 98312 | tf_op jit(solution)/shard_map/ppermute | solution.py:18
  16.7 4.3 %collective-permute-start.1 = (f32[2,1,8,512]{3,2,1,0:T(8,128)S(1)}, f32[2,1,8,512]{3,2,1,0:T(8,128)S(1)}, u32[]{:S(2)}, u32[]{:S(2)}) collective-permute-start(f32[2,1,8,512]{3,2,1,0:T(8,128)S(1)} %get-tuple-element.42), channel_id=1, source_target_pairs={{8,0},{16,8},{24,16},{32,24},{40,32},{48,40},{56,48},{64,56},{72,6... | collective-permute-start | bytes 98312 | tf_op jit(solution)/shard_map/ppermute | solution.py:20
  21.3 5.9 %collective-permute-start.4 = (f32[2,1,8,512]{3,2,1,0:T(8,128)S(1)}, f32[2,1,8,512]{3,2,1,0:T(8,128)S(1)}, u32[]{:S(2)}, u32[]{:S(2)}) collective-permute-start(f32[2,1,8,512]{3,2,1,0:T(8,128)S(1)} %get-tuple-element.40), channel_id=1, source_target_pairs={{0,8},{8,16},{16,24},{24,32},{32,40},{40,48},{48,56},{56,64},{64,7... | collective-permute-start | bytes 98312 | tf_op jit(solution)/shard_map/ppermute | solution.py:18
  25.8 3.1 %collective-permute-start.5 = (f32[2,1,8,512]{3,2,1,0:T(8,128)S(1)}, f32[2,1,8,512]{3,2,1,0:T(8,128)S(1)}, u32[]{:S(2)}, u32[]{:S(2)}) collective-permute-start(f32[2,1,8,512]{3,2,1,0:T(8,128)S(1)} %get-tuple-element.41), channel_id=1, source_target_pairs={{8,0},{16,8},{24,16},{32,24},{40,32},{48,40},{56,48},{64,56},{72,6... | collective-permute-start | bytes 98312 | tf_op jit(solution)/shard_map/ppermute | solution.py:20
  29.3 5.7 %collective-permute-start.6 = (f32[2,1,8,512]{3,2,1,0:T(8,128)S(1)}, f32[2,1,8,512]{3,2,1,0:T(8,128)S(1)}, u32[]{:S(2)}, u32[]{:S(2)}) collective-permute-start(f32[2,1,8,512]{3,2,1,0:T(8,128)S(1)} %get-tuple-element.38), channel_id=1, source_target_pairs={{0,8},{8,16},{16,24},{24,32},{32,40},{40,48},{48,56},{56,64},{64,7... | collective-permute-start | bytes 98312 | tf_op jit(solution)/shard_map/ppermute | solution.py:18
  33.6 3.1 %collective-permute-start.7 = (f32[2,1,8,512]{3,2,1,0:T(8,128)S(1)}, f32[2,1,8,512]{3,2,1,0:T(8,128)S(1)}, u32[]{:S(2)}, u32[]{:S(2)}) collective-permute-start(f32[2,1,8,512]{3,2,1,0:T(8,128)S(1)} %get-tuple-element.39), channel_id=1, source_target_pairs={{8,0},{16,8},{24,16},{32,24},{40,32},{48,40},{56,48},{64,56},{72,6... | collective-permute-start | bytes 98312 | tf_op jit(solution)/shard_map/ppermute | solution.py:20
  37.0 9.6 %copy-start.2 = (s32[16]{0:T(128)S(1)}, s32[16]{0:T(128)}, u32[]{:S(2)}) copy-start(s32[16]{0:T(128)} %param.9) | copy-start | bytes 196
  37.0 5.8 %collective-permute-start.8 = (f32[2,1,8,512]{3,2,1,0:T(8,128)S(1)}, f32[2,1,8,512]{3,2,1,0:T(8,128)S(1)}, u32[]{:S(2)}, u32[]{:S(2)}) collective-permute-start(f32[2,1,8,512]{3,2,1,0:T(8,128)S(1)} %get-tuple-element.36), channel_id=1, source_target_pairs={{0,8},{8,16},{16,24},{24,32},{32,40},{40,48},{48,56},{56,64},{64,7... | collective-permute-start | bytes 98312 | tf_op jit(solution)/shard_map/ppermute | solution.py:18
  41.4 3.1 %collective-permute-start.9 = (f32[2,1,8,512]{3,2,1,0:T(8,128)S(1)}, f32[2,1,8,512]{3,2,1,0:T(8,128)S(1)}, u32[]{:S(2)}, u32[]{:S(2)}) collective-permute-start(f32[2,1,8,512]{3,2,1,0:T(8,128)S(1)} %get-tuple-element.37), channel_id=1, source_target_pairs={{8,0},{16,8},{24,16},{32,24},{40,32},{48,40},{56,48},{64,56},{72,6... | collective-permute-start | bytes 98312 | tf_op jit(solution)/shard_map/ppermute | solution.py:20
  271.3 5.2 %copy-start = (bf16[2,4,8,8,512]{4,3,2,1,0:T(8,128)(2,1)S(1)}, bf16[2,4,8,8,512]{4,3,2,1,0:T(8,128)(2,1)}, u32[]{:S(2)}) copy-start(bf16[2,4,8,8,512]{4,3,2,1,0:T(8,128)(2,1)} %gather_fusion.4) | copy-start | bytes 1572868
  274.5 2.6 copy-start.1
Sparse Core Ops, SparseCore 0:
  46.7 224.5 all-reduce.7
where the time goes:
time: 287 us; the launch traced here: 286 us
  waiting for transfers between devices  208 us (72%)
  local copies, waits for them, and re-layouts  26.4 us (9%)
  starting transfers between devices  26.1 us (9%)
  between operations  13.9 us (5%)
  other arithmetic  11.4 us (4%)
    psum x1, waiting for transfers between devices, spread(): return lax.psum(kept, axis)  201 us
    gather x8, local copies, waits for them, and re-layouts, on_device(): selected = jnp.take(pert_here, chosen, axis=0)  23.7 us
    ppermute x5, starting transfers between devices, with_halo(): lax.ppermute(tail, axis, [(i, (i + 1) % count) for i in range(ends)])  19.7 us
    ppermute x5, waiting for transfers between devices, with_halo(): lax.ppermute(head, axis, [((i + 1) % count, i) for i in range(ends)])  7.04 us
    ppermute x5, starting transfers between devices, with_halo(): lax.ppermute(head, axis, [((i + 1) % count, i) for i in range(ends)])  6.46 us
  transfers between devices with their start and end apart: 11, of which 5 were waited for; matrix products, arithmetic and copies ran while one was open for 9% of the time, Pallas kernels for 0%

commit v1 on v0

--- a/solution.py
+++ b/solution.py
@@ -26,7 +26,7 @@
 
 def spread(value, axis, source):
     kept = jnp.where(lax.axis_index(axis) == source, value, 0).astype(value.dtype)
-    return lax.psum(kept, axis)
+    return jnp.sum(lax.all_gather(kept, axis), axis=0)
 
 
 def weight_sweep(field, coef):

time: 287 us -> 791 us (2.76)
  waiting for transfers between devices: 208 us -> 691 us
  other arithmetic: 11.4 us -> 31.7 us
    all_gather x0 -> x8, waiting for transfers between devices: none -> 680 us  [spread(): return jnp.sum(lax.all_gather(kept, axis), axis=0)]
    psum x1 -> x0, waiting for transfers between devices: 201 us -> none  [spread(): return lax.psum(kept, axis)]
    reduce_sum x0 -> x8, other arithmetic: none -> 13.7 us  [spread(): return jnp.sum(lax.all_gather(kept, axis), axis=0)]
  transfers between devices with their start and end apart: 11 -> 18, of which waited for: 5 -> 12; matrix products, arithmetic and copies ran while one was open for 9% -> 6% of each run, Pallas kernels for 0% -> 0%
where the time goes in v1:
time: 791 us; the launch traced here: 789 us
  waiting for transfers between devices  691 us (87%)
  other arithmetic  31.7 us (4%)
  starting transfers between devices  26.4 us (3%)
  local copies, waits for them, and re-layouts  26.4 us (3%)
  between operations  14 us (2%)
    all_gather x8, waiting for transfers between devices, spread(): return jnp.sum(lax.all_gather(kept, axis), axis=0)  680 us
    gather x8, local copies, waits for them, and re-layouts, on_device(): selected = jnp.take(pert_here, chosen, axis=0)  23.8 us
    ppermute x5, starting transfers between devices, with_halo(): lax.ppermute(tail, axis, [(i, (i + 1) % count) for i in range(ends)])  19.7 us
  transfers between devices with their start and end apart: 18, of which 12 were waited for; matrix products, arithmetic and copies ran while one was open for 6% of the time, Pallas kernels for 0%

profile of v1, /device:TPU:24, one launch (start us, length us, event | category | flops | bytes accessed | tf_op | source)
XLA Modules:
  0.0 789.2 jit_solution(9106036579893977782)
XLA Ops:
  8.1 1.7 collective-permute-start.2
  9.9 1.3 collective-permute-start.3
  11.9 4.7 collective-permute-start
  16.7 1.3 collective-permute-start.1
  18.2 1.0 constant_dynamic-update-slice_fusion.1
  19.2 1.8 collective-permute-done.1
  21.3 4.5 collective-permute-start.4
  25.8 1.3 collective-permute-start.5
  27.2 1.8 collective-permute-done.5
  29.3 4.3 collective-permute-start.6
  33.6 1.3 collective-permute-start.7
  34.9 1.8 collective-permute-done.7
  37.0 4.3 collective-permute-start.8
  41.4 1.3 collective-permute-start.9
  42.8 1.7 collective-permute-done.9
  44.8 0.9 broadcast_select_fusion.6
  45.6 1.0 broadcast_select_fusion.7
  51.4 2.8 gather_fusion
  54.1 2.8 gather_fusion.1
  56.9 2.8 gather_fusion.2
  59.7 2.8 gather_fusion.3
  62.5 2.8 gather_fusion.4
  65.3 2.8 gather_fusion.5
  68.1 3.6 gather_fusion.6
  71.7 3.6 gather_fusion.7
  75.3 104.6 %all-gather.17.cloned.1.call-done = bf16[16,8,8,512]{3,2,1,0:T(8,128)(2,1)} async-done(((bf16[2,8,8,512]{3,2,1,0:T(8,128)(2,1)}), bf16[16,8,8,512]{3,2,1,0:T(8,128)(2,1)}) %all-gather.17.cloned.1.call-update) | async-done | bytes 1048592 | tf_op jit(solution)/shard_map/all_gather | solution.py:29
  179.9 1.4 reduce_sum.96
  181.3 83.8 %all-gather.19.cloned.1.call-done = bf16[16,8,8,512]{3,2,1,0:T(8,128)(2,1)} async-done(((bf16[2,8,8,512]{3,2,1,0:T(8,128)(2,1)}), bf16[16,8,8,512]{3,2,1,0:T(8,128)(2,1)}) %all-gather.19.cloned.1.call-update) | async-done | bytes 1048592 | tf_op jit(solution)/shard_map/all_gather | solution.py:29
  265.0 1.4 reduce_sum.97
  266.4 83.8 %all-gather.23.cloned.1.call-done = bf16[16,8,8,512]{3,2,1,0:T(8,128)(2,1)} async-done(((bf16[2,8,8,512]{3,2,1,0:T(8,128)(2,1)}), bf16[16,8,8,512]{3,2,1,0:T(8,128)(2,1)}) %all-gather.23.cloned.1.call-update) | async-done | bytes 1048592 | tf_op jit(solution)/shard_map/all_gather | solution.py:29
  350.2 1.4 reduce_sum.99
  351.6 83.6 %all-gather.21.cloned.1.call-done = bf16[16,8,8,512]{3,2,1,0:T(8,128)(2,1)} async-done(((bf16[2,8,8,512]{3,2,1,0:T(8,128)(2,1)}), bf16[16,8,8,512]{3,2,1,0:T(8,128)(2,1)}) %all-gather.21.cloned.1.call-update) | async-done | bytes 1048592 | tf_op jit(solution)/shard_map/all_gather | solution.py:29
  435.2 2.1 reduce_sum.98
  437.3 82.9 %all-gather.27.cloned.1.call-done = bf16[16,8,8,512]{3,2,1,0:T(8,128)(2,1)} async-done(((bf16[2,8,8,512]{3,2,1,0:T(8,128)(2,1)}), bf16[16,8,8,512]{3,2,1,0:T(8,128)(2,1)}) %all-gather.27.cloned.1.call-update) | async-done | bytes 1048592 | tf_op jit(solution)/shard_map/all_gather | solution.py:29
  520.2 2.0 reduce_sum.101
  522.3 83.0 %all-gather.25.cloned.1.call-done = bf16[16,8,8,512]{3,2,1,0:T(8,128)(2,1)} async-done(((bf16[2,8,8,512]{3,2,1,0:T(8,128)(2,1)}), bf16[16,8,8,512]{3,2,1,0:T(8,128)(2,1)}) %all-gather.25.cloned.1.call-update) | async-done | bytes 1048592 | tf_op jit(solution)/shard_map/all_gather | solution.py:29
  605.2 2.1 reduce_sum.100
  607.3 83.1 %all-gather.31.cloned.1.call-done = bf16[16,8,8,512]{3,2,1,0:T(8,128)(2,1)} async-done(((bf16[2,8,8,512]{3,2,1,0:T(8,128)(2,1)}), bf16[16,8,8,512]{3,2,1,0:T(8,128)(2,1)}) %all-gather.31.cloned.1.call-update) | async-done | bytes 1048592 | tf_op jit(solution)/shard_map/all_gather | solution.py:29
  690.4 2.1 reduce_sum.103
  694.6 1.6 bitcast_convert_fusion.5
  696.3 1.6 bitcast_convert_fusion.2
  697.9 1.6 bitcast_convert_fusion.3
  699.5 0.9 bitcast_convert_fusion
  700.5 75.1 %all-gather.29.cloned.1.call-done = bf16[16,8,8,512]{3,2,1,0:T(8,128)(2,1)} async-done(((bf16[2,8,8,512]{3,2,1,0:T(8,128)(2,1)}), bf16[16,8,8,512]{3,2,1,0:T(8,128)(2,1)}) %all-gather.29.cloned.1.call-update) | async-done | bytes 1048592 | tf_op jit(solution)/shard_map/all_gather | solution.py:29
  775.5 1.4 reduce_sum.102
  777.0 1.7 multiply_reduce_fusion.6
  778.7 1.6 multiply_reduce_fusion.4
  781.1 1.3 multiply_bitcast_fusion
  (73 shorter events, 11.4 us)
Async XLA Ops:
  6.5 173.4 %all-gather.17.cloned.1.call-start = ((), (), s32[]{:S(2)}) async-start(), calls=%async_computation | async-start | bytes 1179648 | tf_op jit(solution)/shard_map/all_gather | solution.py:29
  8.1 9.9 %collective-permute-start.2 = (f32[1,8,512]{2,1,0:T(8,128)S(1)}, f32[1,8,512]{2,1,0:T(8,128)S(1)}, u32[]{:S(2)}, u32[]{:S(2)}) collective-permute-start(f32[1,8,512]{2,1,0:T(8,128)S(1)} %get-tuple-element.47), channel_id=1, source_target_pairs={{0,8},{8,16},{16,24},{24,32},{32,40},{40,48},{48,56},{56,64},{64,7... | collective-permute-start | bytes 49160 | tf_op jit(solution)/shard_map/ppermute | solution.py:18
  9.9 8.1 %collective-permute-start.3 = (f32[1,8,512]{2,1,0:T(8,128)S(1)}, f32[1,8,512]{2,1,0:T(8,128)S(1)}, u32[]{:S(2)}, u32[]{:S(2)}) collective-permute-start(f32[1,8,512]{2,1,0:T(8,128)S(1)} %get-tuple-element.48), channel_id=1, source_target_pairs={{8,0},{16,8},{24,16},{32,24},{40,32},{48,40},{56,48},{64,56},{72,6... | collective-permute-start | bytes 49160 | tf_op jit(solution)/shard_map/ppermute | solution.py:20
  11.9 6.2 collective-permute-start
  16.7 4.3 collective-permute-start.1
  21.3 5.9 collective-permute-start.4
  25.8 3.1 collective-permute-start.5
  29.3 5.7 collective-permute-start.6
  33.6 3.1 collective-permute-start.7
  37.0 13.7 %copy-start.4 = (s32[16]{0:T(128)S(1)}, s32[16]{0:T(128)}, u32[]{:S(2)}) copy-start(s32[16]{0:T(128)} %param.9) | copy-start | bytes 196
  37.0 5.8 collective-permute-start.8
  41.4 3.1 collective-permute-start.9
  46.7 218.4 %all-gather.19.cloned.1.call-start = ((), (), s32[]{:S(2)}) async-start(), calls=%async_computation.1 | async-start | bytes 1179648 | tf_op jit(solution)/shard_map/all_gather | solution.py:29
  47.4 302.8 %all-gather.23.cloned.1.call-start = ((), (), s32[]{:S(2)}) async-start(), calls=%async_computation.3 | async-start | bytes 1179648 | tf_op jit(solution)/shard_map/all_gather | solution.py:29
  48.2 387.0 %all-gather.21.cloned.1.call-start = ((), (), s32[]{:S(2)}) async-start(), calls=%async_computation.2 | async-start | bytes 1179648 | tf_op jit(solution)/shard_map/all_gather | solution.py:29
  48.8 471.5 %all-gather.27.cloned.1.call-start = ((), (), s32[]{:S(2)}) async-start(), calls=%async_computation.5 | async-start | bytes 1179648 | tf_op jit(solution)/shard_map/all_gather | solution.py:29
  49.3 555.9 %all-gather.25.cloned.1.call-start = ((), (), s32[]{:S(2)}) async-start(), calls=%async_computation.4 | async-start | bytes 1179648 | tf_op jit(solution)/shard_map/all_gather | solution.py:29
  49.9 640.5 %all-gather.31.cloned.1.call-start = ((), (), s32[]{:S(2)}) async-start(), calls=%async_computation.7 | async-start | bytes 1179648 | tf_op jit(solution)/shard_map/all_gather | solution.py:29
  50.7 724.9 %all-gather.29.cloned.1.call-start = ((), (), s32[]{:S(2)}) async-start(), calls=%async_computation.6 | async-start | bytes 1179648 | tf_op jit(solution)/shard_map/all_gather | solution.py:29
  776.9 3.3 copy-start.2
  776.9 3.3 copy-start.3
  776.9 3.7 copy-start
  776.9 3.7 copy-start.1
Sparse Core Ops, SparseCore 0:
  46.8 133.0 all-gather.16
  183.1 81.9 all-gather.18
  268.3 81.9 all-gather.22
  353.3 81.9 all-gather.20
  438.3 81.9 all-gather.26
  523.3 81.9 all-gather.24
  608.4 81.9 all-gather.30
  693.6 81.9 all-gather.28
